TPU v7x, 256 devices: a whole 4x4x8 slice. The times are simulated.
256 devices in a mesh: pb: 16 (over z, core), kv: 16 (over y, x).
Axes of the slice: x: 4, y: 4, z: 8, core: 2. Of those that a mesh axis runs over, the one named last changes fastest.
Arguments:
- queries: bfloat16 [393216, 1024], P(('pb', 'kv')), may hold values from -8 to 8
- keys: bfloat16 [524288, 128], P(('kv', 'pb')), may hold values from -6 to 6
- values: bfloat16 [524288, 128], P(('kv', 'pb')), may hold values from -6 to 6
- selected: int32 [6144, 14], P(('pb', 'kv')), may hold values from 1 to 8190, as said below
Outputs:
- attended: bfloat16 [393216, 1024], P(('pb', 'kv'))
Inputs may be any that keep to these rules, and one draw needn't show every extreme that they name: `selected`: each row names 14 different blocks, never block 0 or block 8191. Key device k holds blocks k * 32 to (k + 1) * 32 - 1, devices counted with kv slowest; query device d holds query blocks d * 24 to (d + 1) * 24 - 1, devices counted with pb slowest. The query blocks of one device name together at most 2 distinct blocks of one key device, and in every draw some key device has exactly 2 named by every query device.
All inputs are finite; a program needn't handle non-finite values.
Results may differ from a plain program's by a relative error of at most 0.0046.
Values may be sent and summed in bfloat16 or wider, within the bound.
A program may use at most 128 MiB of HBM per device.

v0:
```python
import math
import jax
import jax.numpy as jnp
from jax import lax
from jax.sharding import PartitionSpec as P

H = 8
DH = 128
BLOCK = 64
TOPN = 16
QB = 64
CAP = 2


def holdings(wanted, owner, blocks_here):
    local_ids = owner * blocks_here + jnp.arange(blocks_here, dtype=jnp.int32)
    hits = (wanted[:, None] == local_ids[None, :]).astype(jnp.int32)
    present = jnp.max(hits, axis=0)
    return (present, jnp.cumsum(present) - present)


def slot_lists(present, slot_rank, slots):
    local_ids = jnp.arange(present.shape[-1], dtype=jnp.int32)
    slot_ids = jnp.arange(slots, dtype=jnp.int32)
    matches = (present[..., :, None] == 1) & (slot_rank[..., :, None] == slot_ids)
    return jnp.sum(jnp.where(matches, local_ids[:, None], 0), axis=-2)


def per_device(queries, keys, values, selected):
    pb_count = lax.axis_size("pb")
    kv_count = lax.axis_size("kv")
    devices = pb_count * kv_count
    blocks_here = keys.shape[0] // BLOCK
    query_blocks = queries.shape[0] // QB
    column_blocks = pb_count * blocks_here
    tiles_local = jnp.concatenate(
        [keys.reshape(blocks_here, BLOCK, DH), values.reshape(blocks_here, BLOCK, DH)], axis=2
    )
    column = lax.all_gather(tiles_local, "pb", axis=0, tiled=True)
    slots = CAP
    wanted = selected.reshape(-1)
    owners = jnp.arange(devices, dtype=jnp.int32)
    present, slot_rank = jax.vmap(lambda owner: holdings(wanted, owner, blocks_here))(owners)
    owner_lists = slot_lists(present, slot_rank, slots)
    by_column = (
        owner_lists.reshape(kv_count, pb_count, slots)
        + jnp.arange(pb_count, dtype=jnp.int32)[None, :, None] * blocks_here
    )
    by_column = by_column.reshape(kv_count, pb_count * slots)
    asked_for = lax.all_to_all(by_column, "kv", split_axis=0, concat_axis=0, tiled=True)
    outgoing = jnp.take(column, asked_for.reshape(-1), axis=0).reshape(
        kv_count, pb_count * slots, BLOCK, 2 * DH
    )
    fetched = lax.all_to_all(outgoing, "kv", split_axis=0, concat_axis=0, tiled=True)
    tile_table = fetched.reshape(devices * slots, BLOCK, 2 * DH)
    owner_of = selected // blocks_here
    positions = owner_of * slots + jnp.take(slot_rank.reshape(-1), selected)
    me_kv = lax.axis_index("kv")
    ends = jnp.concatenate([column[:1], column[column_blocks - 1 :]], axis=0)
    ends = jnp.where(
        jnp.stack([me_kv == 0, me_kv == kv_count - 1])[:, None, None], ends, jnp.zeros_like(ends)
    )
    ends = lax.psum(ends, "kv")
    tile_table = jnp.concatenate([tile_table, ends], axis=0)
    extra_base = devices * slots
    leading_positions = jnp.broadcast_to(
        jnp.array([extra_base, extra_base + 1], jnp.int32), (query_blocks, 2)
    )
    positions = jnp.concatenate([leading_positions, positions], axis=1)
    group_size = math.gcd(query_blocks, 8)
    q_groups = queries.reshape(query_blocks // group_size, group_size, QB * H, DH)
    p_groups = positions.reshape(query_blocks // group_size, group_size, TOPN)

    def attend(operands):
        q_block, positions_in = operands
        gathered = jnp.take(tile_table, positions_in.reshape(-1), axis=0).reshape(
            group_size, TOPN * BLOCK, 2 * DH
        )
        scores = jnp.einsum(
            "gqd,gkd->gqk", q_block, gathered[..., :DH], preferred_element_type=jnp.float32
        ) * DH ** (-0.5)
        weights = jnp.exp(scores - jnp.max(scores, axis=-1, keepdims=True))
        totals = jnp.sum(weights, axis=-1, keepdims=True)
        weighted = jnp.einsum(
            "gqk,gkd->gqd",
            weights.astype(jnp.bfloat16),
            gathered[..., DH:],
            preferred_element_type=jnp.float32,
        )
        return (weighted / totals).astype(jnp.bfloat16)

    result = lax.map(attend, (q_groups, p_groups))
    return result.reshape(query_blocks * QB, H * DH)


def solution(mesh):
    placed = (
        P(("pb", "kv"), None),
        P(("kv", "pb"), None),
        P(("kv", "pb"), None),
        P(("pb", "kv"), None),
    )
    return jax.shard_map(
        per_device, mesh=mesh, in_specs=placed, out_specs=P(("pb", "kv"), None), check_vma=False
    )
```

profile of v0, /device:TPU:2, one launch (start us, length us, event | category | flops | bytes accessed | tf_op | source)
XLA Modules:
  0.0 519.4 jit_solution(11960891043452149832)
XLA Ops:
  6.5 2.3 pad_maximum_fusion.1
  9.0 0.8 copy.30
  9.9 1.7 convert_reduce_fusion
  12.1 13.5 %all_to_all.11 = s32[16,1,32]{2,1,0:T(1,128)S(1)} all-to-all(s32[16,1,32]{2,1,0:T(1,128)S(1)} %bitcast.44), channel_id=1, replica_groups=mesh['pb'=16,'kv'=16] {'kv'}, dimensions={0} | all-to-all | bytes 4096 | tf_op jit(solution)/shard_map/all_to_all | solution.py:50
  26.0 0.6 reduce.3
  26.7 80.8 %all-gather.2.cloned.1.call-done = bf16[512,64,256]{2,1,0:T(8,128)(2,1)} async-done(((bf16[32,64,256]{2,1,0:T(8,128)(2,1)}), bf16[512,64,256]{2,1,0:T(8,128)(2,1)}) %all-gather.2.cloned.1.call-update) | async-done | bytes 16777232 | tf_op jit(solution)/shard_map/all_gather | solution.py:39
  107.6 19.5 %gather_fusion.2 = bf16[512,64,256]{2,1,0:T(8,128)(2,1)} fusion(bf16[512,64,256]{2,1,0:T(8,128)(2,1)} %all-gather.2.cloned.1.call-done, s32[1024]{0:T(1024)S(1)} %pad_clamp_fusion.1), kind=kCustom, calls=%fused_computation.2 | custom fusion | bytes 33556480 | tf_op jit(solution)/shard_map/jit(_take)/gather | solution.py:51
  127.0 14.1 %broadcast_select_fusion = bf16[16,32,64,256]{3,2,1,0:T(8,128)(2,1)} fusion(bf16[16,32,64,256]{3,2,1,0:T(8,128)(2,1)} %bitcast.40, pred[16,32]{1,0:T(8,128)(4,1)S(1)} %compare_and_fusion.1), kind=kLoop, calls=%fused_computation.27 | loop fusion | flops 8388608 | bytes 33554944 | tf_op jit(solution)/shard_map/jit(_take)/select_n | solution.py:51
  141.2 7.4 %all-to-all-start.1 = ((bf16[16,32,64,256]{3,2,1,0:T(8,128)(2,1)}), bf16[16,32,64,256]{3,2,1,0:T(8,128)(2,1)}, u32[]{:S(2)}, u32[]{:S(2)}) async-start(bf16[16,32,64,256]{3,2,1,0:T(8,128)(2,1)} %broadcast_select_fusion), calls=%async_computation.1 | async-start | bytes 33554432 | tf_op jit(solution)/shard_map/all_to_all | solution.py:54
  149.0 2.5 gather_fusion.1
  151.7 0.8 fusion.23
  152.5 0.7 maximum_select_fusion
  153.3 4.1 reshape.203
  157.4 264.4 %all-reduce.2.cloned.1.call-done = bf16[2,64,256]{2,1,0:T(8,128)(2,1)} async-done(((bf16[2,64,256]{2,1,0:T(8,128)(2,1)}), bf16[2,64,256]{2,1,0:T(8,128)(2,1)}) %all-reduce.2.cloned.1.call-update) | async-done | bytes 65552 | tf_op jit(solution)/shard_map/psum | solution.py:63
  421.9 14.1 %pad_maximum_fusion = bf16[514,64,256]{2,1,0:T(8,128)(2,1)} fusion(bf16[2,64,256]{2,1,0:T(8,128)(2,1)} %all-reduce.2.cloned.1.call-done, bf16[512,64,256]{2,1,0:T(8,128)(2,1)} %bitcast.12), kind=kLoop, calls=%fused_computation.26 | loop fusion | flops 8421376 | bytes 33685504 | tf_op jit(solution)/shard_map/concatenate | solution.py:64
  436.0 70.9 %while.10 = (s32[]{:T(128)}, bf16[3,8,512,128]{3,2,1,0:T(8,128)(2,1)}, bf16[3,8,512,128]{3,2,1,0:T(8,128)(2,1)S(1)}, s32[3,8,16]{2,1,0:T(8,128)S(1)}, bf16[514,64,256]{2,1,0:T(8,128)(2,1)}, /*index=5*/s32[]{:T(128)}) while((s32[]{:T(128)}, bf16[3,8,512,128]{3,2,1,0:T(8,128)(2,1)}, bf16[3,8,512,128]{3,2,1,0:T(8,128)(2,1)S(1)}, ...), condition=%wide.region_7.8_spmd, body=%wide.region_4.7_spmd.sunk | while | flops 2184177664 | bytes 73523544 | solution.py:92
  436.3 8.5 %gather_fusion = bf16[128,64,256]{2,1,0:T(8,128)(2,1)} fusion(bf16[514,64,256]{2,1,0:T(8,128)(2,1)} %get-tuple-element.104, s32[1024]{0:T(1024)S(1)} %pad_clamp_fusion.4), kind=kCustom, calls=%fused_computation.clone.1 | custom fusion | bytes 8389120 | tf_op jit(solution)/shard_map/while/body/eval_jaxpr/jit(_take)/gather | solution.py:76
  444.8 4.6 bitcast_select_fusion.2
  449.4 2.4 multiply_reduce_fusion.2
  451.8 3.5 fusion.31
  455.3 4.2 bitcast_dynamic-update-slice_fusion.2
  459.9 8.5 %gather_fusion = bf16[128,64,256]{2,1,0:T(8,128)(2,1)} fusion(bf16[514,64,256]{2,1,0:T(8,128)(2,1)} %get-tuple-element.104, s32[1024]{0:T(1024)S(1)} %pad_clamp_fusion.4), kind=kCustom, calls=%fused_computation.clone.1 | custom fusion | bytes 8389120 | tf_op jit(solution)/shard_map/while/body/eval_jaxpr/jit(_take)/gather | solution.py:76
  468.4 4.6 bitcast_select_fusion.2
  473.0 2.4 multiply_reduce_fusion.2
  475.4 3.5 fusion.31
  479.0 4.2 bitcast_dynamic-update-slice_fusion.2
  483.5 8.5 %gather_fusion = bf16[128,64,256]{2,1,0:T(8,128)(2,1)} fusion(bf16[514,64,256]{2,1,0:T(8,128)(2,1)} %get-tuple-element.104, s32[1024]{0:T(1024)S(1)} %pad_clamp_fusion.4), kind=kCustom, calls=%fused_computation.clone.1 | custom fusion | bytes 8389120 | tf_op jit(solution)/shard_map/while/body/eval_jaxpr/jit(_take)/gather | solution.py:76
  492.0 4.6 bitcast_select_fusion.2
  496.6 2.4 multiply_reduce_fusion.2
  499.0 3.5 fusion.31
  502.6 4.2 bitcast_dynamic-update-slice_fusion.2
  506.8 5.8 %reshape.211 = bf16[1536,1024]{1,0:T(8,128)(2,1)} reshape(bf16[3,8,512,128]{3,2,1,0:T(8,128)(2,1)} %get-tuple-element.32) | data formatting | bytes 6291456 | tf_op jit(solution)/shard_map/reshape | solution.py:93
  (54 shorter events, 2.7 us)
Async XLA Ops:
  6.5 101.0 %all-gather.2.cloned.1.call-start = ((), (), s32[]{:S(2)}) async-start(), calls=%async_computation.2 | async-start | bytes 17825792 | tf_op jit(solution)/shard_map/all_gather | solution.py:39
  141.2 7.5 %copy-start = (s32[2]{0:T(128)S(1)}, s32[2]{0:T(128)}, u32[]{:S(2)}) copy-start(s32[2]{0:T(128)} %constant.100.clone) | copy-start | bytes 28
  141.2 280.7 %all-to-all-start.1 = ((bf16[16,32,64,256]{3,2,1,0:T(8,128)(2,1)}), bf16[16,32,64,256]{3,2,1,0:T(8,128)(2,1)}, u32[]{:S(2)}, u32[]{:S(2)}) async-start(bf16[16,32,64,256]{3,2,1,0:T(8,128)(2,1)} %broadcast_select_fusion), calls=%async_computation.1 | async-start | bytes 33554432 | tf_op jit(solution)/shard_map/all_to_all | solution.py:54
  148.6 273.3 %all-reduce.2.cloned.1.call-start = ((), (), s32[]{:S(2)}) async-start(), calls=%async_computation.3 | async-start | bytes 131072 | tf_op jit(solution)/shard_map/psum | solution.py:63
Sparse Core Ops, SparseCore 0:
  9.2 98.3 all-gather.1
  153.3 268.4 all-reduce.1
where the time goes:
time: 521 us; the launch traced here: 519 us
  waiting for transfers between devices  345 us (66%)
  local copies, waits for them, and re-layouts  61.3 us (12%)
  other arithmetic  58.3 us (11%)
  matrix products  20 us (4%)
  between operations  13.6 us (3%)
  blocking collectives  13.5 us (3%)
  starting transfers between devices  7.43 us (1%)
    psum x1, waiting for transfers between devices, per_device(): ends = lax.psum(ends, 'kv')  264 us
    all_gather x1, waiting for transfers between devices, per_device(): column = lax.all_gather(tiles_local, 'pb', axis=0, tiled=True)  80.8 us
    gather x3, local copies, waits for them, and re-layouts, attend(): jnp.take(tile_table, positions_in.reshape(-1), axis=0)  25.6 us
    gather x1, local copies, waits for them, and re-layouts, per_device(): jnp.take(column, asked_for.reshape(-1), axis=0)  19.5 us
    select_n x2, other arithmetic, per_device(): jnp.take(column, asked_for.reshape(-1), axis=0)  14.1 us
    concatenate x1, other arithmetic, per_device(): tile_table = jnp.concatenate([tile_table, ends], axis=0)  14.1 us
    select_n x6, other arithmetic, attend(): jnp.take(tile_table, positions_in.reshape(-1), axis=0)  13.7 us
    all_to_all x1, blocking collectives, per_device(): lax.all_to_all(by_column, 'kv', split_axis=0, concat_axis=0, tiled=True)  13.5 us
  transfers between devices with their start and end apart: 3, of which 2 were waited for; matrix products, arithmetic and copies ran while one was open for 3% of the time, Pallas kernels for 0%

commit v1 on v0

--- a/solution.py
+++ b/solution.py
@@ -60,7 +60,8 @@
     ends = jnp.where(
         jnp.stack([me_kv == 0, me_kv == kv_count - 1])[:, None, None], ends, jnp.zeros_like(ends)
     )
-    ends = lax.psum(ends, "kv")
+    blocks = lax.all_gather(ends, "kv", axis=0, tiled=False)
+    ends = blocks.sum(axis=0)
     tile_table = jnp.concatenate([tile_table, ends], axis=0)
     extra_base = devices * slots
     leading_positions = jnp.broadcast_to(

time: 521 us -> 504 us (0.967); the launches traced: 519 us -> 496 us
  waiting for transfers between devices: 345 us -> 320 us
    psum x1 -> x0, waiting for transfers between devices: 264 us -> none  [per_device(): ends = lax.psum(ends, 'kv')]
    all_gather x0 -> x1, waiting for transfers between devices: none -> 221 us  [per_device(): blocks = lax.all_gather(ends, 'kv', axis=0, tiled=False)]
    all_to_all x1, waiting for transfers between devices: 0.01 us -> 18.9 us  [per_device(): lax.all_to_all(outgoing, 'kv', split_axis=0, concat_axis=0, tiled=True)]
  transfers between devices with their start and end apart: 3 -> 3, of which waited for: 2 -> 3; matrix products, arithmetic and copies ran while one was open for 3% -> 3% of each run, Pallas kernels for 0% -> 0%
where the time goes in v1:
time: 504 us; the launch traced here: 496 us
  waiting for transfers between devices  320 us (63%)
  local copies, waits for them, and re-layouts  61.3 us (12%)
  other arithmetic  59.6 us (12%)
  matrix products  20 us (4%)
  between operations  13.6 us (3%)
  blocking collectives  13.5 us (3%)
  starting transfers between devices  7.43 us (1%)
    all_gather x1, waiting for transfers between devices, per_device(): blocks = lax.all_gather(ends, 'kv', axis=0, tiled=False)  221 us
    all_gather x1, waiting for transfers between devices, per_device(): column = lax.all_gather(tiles_local, 'pb', axis=0, tiled=True)  80.8 us
    gather x3, local copies, waits for them, and re-layouts, attend(): jnp.take(tile_table, positions_in.reshape(-1), axis=0)  25.6 us
    gather x1, local copies, waits for them, and re-layouts, per_device(): jnp.take(column, asked_for.reshape(-1), axis=0)  19.5 us
    all_to_all x1, waiting for transfers between devices, per_device(): lax.all_to_all(outgoing, 'kv', split_axis=0, concat_axis=0, tiled=True)  18.9 us
    select_n x2, other arithmetic, per_device(): jnp.take(column, asked_for.reshape(-1), axis=0)  14.1 us
    concatenate x1, other arithmetic, per_device(): tile_table = jnp.concatenate([tile_table, ends], axis=0)  14 us
    select_n x6, other arithmetic, attend(): jnp.take(tile_table, positions_in.reshape(-1), axis=0)  13.7 us
  transfers between devices with their start and end apart: 3, of which 3 were waited for; matrix products, arithmetic and copies ran while one was open for 3% of the time, Pallas kernels for 0%

profile of v1, /device:TPU:2, one launch (start us, length us, event | category | flops | bytes accessed | tf_op | source)
XLA Modules:
  0.0 495.9 jit_solution(17721883774798702279)
XLA Ops:
  6.5 2.3 pad_maximum_fusion.1
  9.0 0.8 copy.30
  9.9 1.7 convert_reduce_fusion
  12.1 13.5 %all_to_all.11 = s32[16,1,32]{2,1,0:T(1,128)S(1)} all-to-all(s32[16,1,32]{2,1,0:T(1,128)S(1)} %bitcast.48), channel_id=1, replica_groups=mesh['pb'=16,'kv'=16] {'kv'}, dimensions={0} | all-to-all | bytes 4096 | tf_op jit(solution)/shard_map/all_to_all | solution.py:50
  26.7 80.8 %all-gather.3.cloned.1.call-done = bf16[512,64,256]{2,1,0:T(8,128)(2,1)} async-done(((bf16[32,64,256]{2,1,0:T(8,128)(2,1)}), bf16[512,64,256]{2,1,0:T(8,128)(2,1)}) %all-gather.3.cloned.1.call-update) | async-done | bytes 16777232 | tf_op jit(solution)/shard_map/all_gather | solution.py:39
  107.6 19.5 %gather_fusion.2 = bf16[512,64,256]{2,1,0:T(8,128)(2,1)} fusion(bf16[512,64,256]{2,1,0:T(8,128)(2,1)} %all-gather.3.cloned.1.call-done, s32[1024]{0:T(1024)S(1)} %pad_clamp_fusion.1), kind=kCustom, calls=%fused_computation.2 | custom fusion | bytes 33556480 | tf_op jit(solution)/shard_map/jit(_take)/gather | solution.py:51
  127.0 14.1 %broadcast_select_fusion = bf16[16,32,64,256]{3,2,1,0:T(8,128)(2,1)} fusion(bf16[16,32,64,256]{3,2,1,0:T(8,128)(2,1)} %bitcast.44, pred[16,32]{1,0:T(8,128)(4,1)S(1)} %compare_and_fusion.1), kind=kLoop, calls=%fused_computation.27 | loop fusion | flops 8388608 | bytes 33554944 | tf_op jit(solution)/shard_map/jit(_take)/select_n | solution.py:51
  141.2 7.4 %all-to-all-start.1 = ((bf16[16,32,64,256]{3,2,1,0:T(8,128)(2,1)}), bf16[16,32,64,256]{3,2,1,0:T(8,128)(2,1)}, u32[]{:S(2)}, u32[]{:S(2)}) async-start(bf16[16,32,64,256]{3,2,1,0:T(8,128)(2,1)} %broadcast_select_fusion), calls=%async_computation.1 | async-start | bytes 33554432 | tf_op jit(solution)/shard_map/all_to_all | solution.py:54
  148.7 0.8 slice_bitcast_fusion.1
  150.6 2.5 gather_fusion.1
  153.2 4.1 reshape.232
  157.4 220.7 %all-gather.5.cloned.1.call-done = bf16[16,2,64,256]{3,2,1,0:T(8,128)(2,1)} async-done(((bf16[1,2,64,256]{3,2,1,0:T(8,128)(2,1)}), bf16[16,2,64,256]{3,2,1,0:T(8,128)(2,1)}) %all-gather.5.cloned.1.call-update) | async-done | bytes 1048592 | tf_op jit(solution)/shard_map/all_gather | solution.py:63
  378.2 1.4 reduce_sum.31
  379.5 18.9 %all-to-all-done.1 = bf16[16,32,64,256]{3,2,1,0:T(8,128)(2,1)} async-done(((bf16[16,32,64,256]{3,2,1,0:T(8,128)(2,1)}), bf16[16,32,64,256]{3,2,1,0:T(8,128)(2,1)}, u32[]{:S(2)}, u32[]{:S(2)}) %all-to-all-start.1) | async-done | bytes 16777248 | tf_op jit(solution)/shard_map/all_to_all | solution.py:54
  398.4 14.0 %pad_maximum_fusion = bf16[514,64,256]{2,1,0:T(8,128)(2,1)} fusion(bf16[2,64,256]{2,1,0:T(8,128)(2,1)S(1)} %reduce_sum.31, bf16[512,64,256]{2,1,0:T(8,128)(2,1)} %bitcast.12), kind=kLoop, calls=%fused_computation.26 | loop fusion | flops 8421376 | bytes 33685504 | tf_op jit(solution)/shard_map/concatenate | solution.py:65
  412.4 70.9 %while.10 = (s32[]{:T(128)}, bf16[3,8,512,128]{3,2,1,0:T(8,128)(2,1)}, bf16[3,8,512,128]{3,2,1,0:T(8,128)(2,1)S(1)}, s32[3,8,16]{2,1,0:T(8,128)S(1)}, bf16[514,64,256]{2,1,0:T(8,128)(2,1)}, /*index=5*/s32[]{:T(128)}) while((s32[]{:T(128)}, bf16[3,8,512,128]{3,2,1,0:T(8,128)(2,1)}, bf16[3,8,512,128]{3,2,1,0:T(8,128)(2,1)S(1)}, ...), condition=%wide.region_7.8_spmd, body=%wide.region_4.7_spmd.sunk | while | flops 2184177664 | bytes 73523544 | solution.py:93
  412.7 8.5 %gather_fusion = bf16[128,64,256]{2,1,0:T(8,128)(2,1)} fusion(bf16[514,64,256]{2,1,0:T(8,128)(2,1)} %get-tuple-element.104, s32[1024]{0:T(1024)S(1)} %pad_clamp_fusion.4), kind=kCustom, calls=%fused_computation.clone.1 | custom fusion | bytes 8389120 | tf_op jit(solution)/shard_map/while/body/eval_jaxpr/jit(_take)/gather | solution.py:77
  421.3 4.6 bitcast_select_fusion.2
  425.8 2.4 multiply_reduce_fusion.2
  428.3 3.5 fusion.30
  431.8 4.2 bitcast_dynamic-update-slice_fusion.2
  436.3 8.5 %gather_fusion = bf16[128,64,256]{2,1,0:T(8,128)(2,1)} fusion(bf16[514,64,256]{2,1,0:T(8,128)(2,1)} %get-tuple-element.104, s32[1024]{0:T(1024)S(1)} %pad_clamp_fusion.4), kind=kCustom, calls=%fused_computation.clone.1 | custom fusion | bytes 8389120 | tf_op jit(solution)/shard_map/while/body/eval_jaxpr/jit(_take)/gather | solution.py:77
  444.9 4.6 bitcast_select_fusion.2
  449.5 2.4 multiply_reduce_fusion.2
  451.9 3.5 fusion.30
  455.4 4.2 bitcast_dynamic-update-slice_fusion.2
  460.0 8.5 %gather_fusion = bf16[128,64,256]{2,1,0:T(8,128)(2,1)} fusion(bf16[514,64,256]{2,1,0:T(8,128)(2,1)} %get-tuple-element.104, s32[1024]{0:T(1024)S(1)} %pad_clamp_fusion.4), kind=kCustom, calls=%fused_computation.clone.1 | custom fusion | bytes 8389120 | tf_op jit(solution)/shard_map/while/body/eval_jaxpr/jit(_take)/gather | solution.py:77
  468.5 4.6 bitcast_select_fusion.2
  473.1 2.4 multiply_reduce_fusion.2
  475.5 3.5 fusion.30
  479.0 4.2 bitcast_dynamic-update-slice_fusion.2
  483.3 5.8 %reshape.240 = bf16[1536,1024]{1,0:T(8,128)(2,1)} reshape(bf16[3,8,512,128]{3,2,1,0:T(8,128)(2,1)} %get-tuple-element.32) | data formatting | bytes 6291456 | tf_op jit(solution)/shard_map/reshape | solution.py:94
  (55 shorter events, 4.0 us)
Async XLA Ops:
  6.5 101.0 %all-gather.3.cloned.1.call-start = ((), (), s32[]{:S(2)}) async-start(), calls=%async_computation.2 | async-start | bytes 17825792 | tf_op jit(solution)/shard_map/all_gather | solution.py:39
  141.2 9.1 %copy-start = (s32[2]{0:T(128)S(1)}, s32[2]{0:T(128)}, u32[]{:S(2)}) copy-start(s32[2]{0:T(128)} %constant.102.clone) | copy-start | bytes 28
  141.2 257.2 %all-to-all-start.1 = ((bf16[16,32,64,256]{3,2,1,0:T(8,128)(2,1)}), bf16[16,32,64,256]{3,2,1,0:T(8,128)(2,1)}, u32[]{:S(2)}, u32[]{:S(2)}) async-start(bf16[16,32,64,256]{3,2,1,0:T(8,128)(2,1)} %broadcast_select_fusion), calls=%async_computation.1 | async-start | bytes 33554432 | tf_op jit(solution)/shard_map/all_to_all | solution.py:54
  148.6 229.6 %all-gather.5.cloned.1.call-start = ((), (), s32[]{:S(2)}) async-start(), calls=%async_computation.3 | async-start | bytes 1114112 | tf_op jit(solution)/shard_map/all_gather | solution.py:63
Sparse Core Ops, SparseCore 0:
  9.2 98.3 all-gather.2
  151.8 226.2 all-gather.4
